TPU v7x, 32 devices: a whole 2x2x4 slice. The times are simulated.
32 devices in a mesh: tile: 16 (over z, x, core), group: 2 (over y).
Axes of the slice: x: 2, y: 2, z: 4, core: 2. Of those that a mesh axis runs over, the one named last changes fastest.
Arguments:
- object_field: float32 [2, 320, 2048], P(None, 'group', 'tile'), may hold values from -6 to 6
- probe_field: float32 [2, 256, 256], replicated, may hold values from -6 to 6
- amplitudes: float32 [32, 256, 256], P(('tile', 'group')), may hold values from 0 to 4
- row_start: int32 [32], P(('tile', 'group')), may hold values from 0 to 64
- column_start: int32 [32], P(('tile', 'group')), may hold values from 0 to 128
- live_slots: int32 [32], P(('tile', 'group')), may hold values 0 or 1
Outputs:
- new_object: float32 [2, 320, 2048], P(None, 'group', 'tile')
- new_probe: float32 [2, 256, 256], replicated
All inputs are finite; a program needn't handle non-finite values. No bound on the sum of `live_slots` on one device may be relied on, other than what follows from the above.
Results may differ from a plain program's by a relative error of at most 0.0001.
Values sent between devices are 32-bit elements; how exact they have to be, the bound alone decides.
A program may use at most 64 MiB of HBM per device.

v0:
```python
import math
import jax
import jax.numpy as jnp
from jax import lax
from jax.sharding import PartitionSpec as P

WIN = 256
HALO = 128


def padded_2(value, sides, width):
    for axis, dim in sides:
        count, length = (lax.axis_size(axis), value.shape[dim])
        up = [(i, (i + 1) % count) for i in range(count - 1)]
        down = [(j, i) for i, j in up]
        last = lax.slice_in_dim(value, length - width, length, axis=dim)
        initial = lax.slice_in_dim(value, 0, width, axis=dim)
        before = lax.ppermute(last, axis, up)
        after = lax.ppermute(initial, axis, down)
        value = jnp.concatenate([before, value, after], axis=dim)
    return value


def dft_tables(length):
    counter = jnp.arange(length, dtype=jnp.int32)
    product = counter[:, None] * counter[None, :] % length
    angles = 2.0 * math.pi / length * product.astype(jnp.float32)
    factor = 1.0 / math.sqrt(length)
    return (jnp.cos(angles) * factor, jnp.sin(angles) * factor)


def apply_left(matrix, values):
    return jnp.einsum("jk,pkl->pjl", matrix, values, precision=lax.Precision.HIGHEST)


def apply_right(values, matrix):
    return jnp.einsum("pjk,kl->pjl", values, matrix, precision=lax.Precision.HIGHEST)


def transform(real_part, imag_part, cos_table, sin_table, sign):
    left_real = apply_left(cos_table, real_part) - sign * apply_left(sin_table, imag_part)
    left_imag = apply_left(cos_table, imag_part) + sign * apply_left(sin_table, real_part)
    right_real = apply_right(left_real, cos_table) - sign * apply_right(left_imag, sin_table)
    right_imag = apply_right(left_imag, cos_table) + sign * apply_right(left_real, sin_table)
    return (right_real, right_imag)


def window_terms(windows, probe_field, amplitudes, live_slots, cos_table, sin_table):
    sample_real = windows[:, 0]
    sample_imag = windows[:, 1]
    probe_real = probe_field[0]
    probe_imag = probe_field[1]
    exit_real = probe_real * sample_real - probe_imag * sample_imag
    exit_imag = probe_real * sample_imag + probe_imag * sample_real
    far_real, far_imag = transform(exit_real, exit_imag, cos_table, sin_table, -1.0)
    modulus = jnp.maximum(jnp.sqrt(far_real * far_real + far_imag * far_imag), 0.25)
    factor = 1.0 - amplitudes / modulus
    miss_real, miss_imag = transform(
        far_real * factor, far_imag * factor, cos_table, sin_table, 1.0
    )
    weight = live_slots.astype(jnp.float32)[:, None, None]
    miss_real = miss_real * weight
    miss_imag = miss_imag * weight
    grad_real = probe_real * miss_real + probe_imag * miss_imag
    grad_imag = probe_real * miss_imag - probe_imag * miss_real
    probe_light = weight * (probe_real * probe_real + probe_imag * probe_imag)
    terms = jnp.stack([grad_real, grad_imag, probe_light], axis=1)
    probe_grad = jnp.stack(
        [
            jnp.sum(sample_real * miss_real + sample_imag * miss_imag, axis=0),
            jnp.sum(sample_real * miss_imag - sample_imag * miss_real, axis=0),
        ],
        axis=0,
    )
    window_light = jnp.sum(weight * (sample_real * sample_real + sample_imag * sample_imag), axis=0)
    return (terms, probe_grad, window_light)


def add_windows(accum, terms, top_rows, left_edges):
    zero_index = jnp.zeros((), jnp.int32)
    channels = terms.shape[1]

    def place(slot, current):
        corner = (zero_index, top_rows[slot], left_edges[slot])
        piece = lax.dynamic_slice(current, corner, (channels, WIN, WIN))
        return lax.dynamic_update_slice(current, piece + terms[slot], corner)

    return lax.fori_loop(0, terms.shape[0], place, accum)


def cut_windows(padded, top_rows, left_edges):
    zero_index = jnp.zeros((), jnp.int32)

    def single(top_row, left_edge):
        return lax.dynamic_slice(padded, (zero_index, top_row, left_edge), (2, WIN, WIN))

    return jax.vmap(single)(top_rows, left_edges)


def edge_strips(accum):
    return jnp.concatenate([accum[:, :, :HALO], accum[:, :, accum.shape[2] - HALO :]], axis=2)


def add_edges(inner, arrived):
    width = inner.shape[2]
    inner = inner.at[:, :, :HALO].add(arrived[:, :, :HALO])
    return inner.at[:, :, width - HALO :].add(arrived[:, :, arrived.shape[2] - HALO :])


def apply_updates(object_field, probe_field, share, probe_grad, window_light):
    light_max = jnp.max(probe_field[0] * probe_field[0] + probe_field[1] * probe_field[1]) + 1e-06
    new_object = object_field - share[0:2] / (share[2:3] + 0.25 * light_max)
    new_probe = (
        probe_field - probe_grad / (window_light + 0.25 * jnp.mean(window_light) + 1e-05)[None]
    )
    return (new_object, new_probe)


def local(object_field, probe_field, amplitudes, row_start, column_start, live_slots):
    cos_table, sin_table = dft_tables(WIN)
    full_rows = lax.all_gather(object_field, "group", axis=1, tiled=True)
    padded = padded_2(full_rows, (("tile", 2),), HALO)
    windows = cut_windows(padded, row_start, column_start)
    terms, probe_grad, window_light = window_terms(
        windows, probe_field, amplitudes, live_slots, cos_table, sin_table
    )
    accum = jnp.zeros((terms.shape[1], padded.shape[1], padded.shape[2]), jnp.float32)
    accum = add_windows(accum, terms, row_start, column_start)
    reduced = lax.psum_scatter(accum, "group", scatter_dimension=1, tiled=True)
    arrived = padded_2(edge_strips(reduced), (("tile", 2),), HALO)
    share = add_edges(reduced[:, :, HALO : reduced.shape[2] - HALO], arrived)
    probe_grad, window_light = lax.psum((probe_grad, window_light), ("tile", "group"))
    object_field, probe_field = apply_updates(
        object_field, probe_field, share, probe_grad, window_light
    )
    return (object_field, probe_field)


def solution(mesh):
    return jax.shard_map(
        local,
        mesh=mesh,
        in_specs=(
            P(None, "group", "tile"),
            P(),
            P(("tile", "group"), None, None),
            P(("tile", "group")),
            P(("tile", "group")),
            P(("tile", "group")),
        ),
        out_specs=(P(None, "group", "tile"), P()),
        check_vma=False,
    )
```

profile of v0, /device:TPU:3, one launch (start us, length us, event | category | flops | bytes accessed | tf_op | source)
XLA Modules:
  0.0 209.8 jit_solution(13786938275999001730)
XLA Ops:
  8.0 0.0 copy-start.1
  8.0 0.0 all-reduce.3.cloned.1.call-start
  8.1 6.1 %all_gather.3 = f32[2,320,128]{2,1,0:T(8,128)S(1)} all-gather(f32[2,160,128]{2,1,0:T(8,128)} %param.14), channel_id=1, replica_groups=mesh['tile'=16,'group'=2] {'group'}, dimensions={1}, use_global_device_ids=true | all-gather | bytes 491520 | tf_op jit(solution)/shard_map/all_gather | solution.py:121
  14.1 3.4 %collective-permute-start.1 = (f32[2,320,128]{2,1,0:T(8,128)S(1)}, f32[2,320,128]{2,1,0:T(8,128)S(1)}, u32[]{:S(2)}, u32[]{:S(2)}) collective-permute-start(f32[2,320,128]{2,1,0:T(8,128)S(1)} %all_gather.3), channel_id=1, source_target_pairs={{2,0},{4,2},{6,4},{8,6},{10,8},{12,10},{14,12},{16,14},{18,16},{20... | collective-permute-start | bytes 983048 | tf_op jit(solution)/shard_map/ppermute | solution.py:19
  17.6 3.1 %collective-permute-start = (f32[2,320,128]{2,1,0:T(8,128)S(1)}, f32[2,320,128]{2,1,0:T(8,128)S(1)}, u32[]{:S(2)}, u32[]{:S(2)}) collective-permute-start(f32[2,320,128]{2,1,0:T(8,128)S(1)} %all_gather.3), channel_id=1, source_target_pairs={{0,2},{2,4},{4,6},{6,8},{8,10},{10,12},{12,14},{14,16},{16,18},{18... | collective-permute-start | bytes 983048 | tf_op jit(solution)/shard_map/ppermute | solution.py:18
  22.6 1.0 collective-permute-done.1
  23.6 1.1 collective-permute-done
  24.7 0.4 fusion.12
  25.1 0.0 copy-done.1
  25.1 0.1 fusion.39
  25.2 1.5 fusion.37
  26.7 1.5 fusion.33
  28.2 1.5 fusion.9
  29.6 1.5 fusion.7
  31.1 1.5 fusion.48
  32.6 0.0 copy-start.4
  32.6 1.5 fusion.49
  34.1 1.5 fusion.4
  35.6 0.0 copy-done.4
  35.6 1.7 bitcast_multiply_fusion.11
  37.4 1.5 fusion.30
  38.8 1.5 fusion.26
  40.3 1.5 fusion.3
  41.8 1.5 fusion.2
  43.3 1.5 fusion.46
  44.8 1.5 fusion.47
  46.3 1.5 fusion
  47.8 1.7 fusion.1
  49.5 0.8 fusion.17
  50.3 0.8 pad_maximum_fusion
  51.1 0.0 all-reduce.3.cloned.1.call-update
  51.1 0.0 reduce-scatter.2.cloned.1.call-start
  51.2 0.7 fusion.23
  51.9 0.1 maximum_bitcast_fusion
  51.9 0.1 broadcast_in_dim.6
  52.0 9.9 %dynamic_update_slice.4 = f32[3,320,384]{2,1,0:T(8,128)S(1)} dynamic-update-slice(f32[3,320,384]{2,1,0:T(8,128)S(1)} %broadcast_in_dim.6, f32[3,256,256]{2,1,0:T(8,128)S(1)} %maximum_bitcast_fusion, s32[]{:T(128)} %constant.112.clone.1, s32[]{:T(128)S(6)} %select_n.60, s32[]{:T(128)S(6)} %select_n.61) | dynamic-update-slice | bytes 1572868 | tf_op jit(solution)/shard_map/while/body/eval_jaxpr/dynamic_update_slice | solution.py:86
  61.9 0.0 copy-start
  61.9 1.1 copy-done
  63.0 0.0 reduce-scatter.2.cloned.1.call-update
  63.7 119.6 %all-reduce.3.cloned.1.call-done = (f32[2,256,256]{2,1,0:T(8,128)}, f32[256,256]{1,0:T(8,128)}) async-done(((f32[2,256,256]{2,1,0:T(8,128)}, f32[256,256]{1,0:T(8,128)}), (f32[2,256,256]{2,1,0:T(8,128)}, f32[256,256]{1,0:T(8,128)})) %all-reduce.3.cloned.1.call-update) | async-done | bytes 786448 | tf_op jit(solution)/shard_map/psum | solution.py:132
  183.3 0.0 copy-start.3
  183.3 1.7 reduce_sum.8
  185.6 1.0 add_add_fusion
  186.6 0.0 reduce-scatter.2.cloned.1.call-done
  186.6 1.1 fusion.132
  187.7 4.5 %collective-permute-start.2 = (f32[3,160,128]{2,1,0:T(8,128)S(1)}, f32[3,160,128]{2,1,0:T(8,128)S(1)}, u32[]{:S(2)}, u32[]{:S(2)}) collective-permute-start(f32[3,160,128]{2,1,0:T(8,128)S(1)} %get-tuple-element.81), channel_id=1, source_target_pairs={{0,2},{2,4},{4,6},{6,8},{8,10},{10,12},{12,14},{14,16},{16,18},{18... | collective-permute-start | bytes 737288 | tf_op jit(solution)/shard_map/ppermute | solution.py:18
  192.2 1.9 collective-permute-start.3
  194.1 0.0 copy-done.3
  194.1 0.0 copy-start.2
  194.2 0.9 divide_subtract_fusion
  195.0 0.3 collective-permute-done.2
  195.3 5.3 %collective-permute-done.3 = f32[3,160,128]{2,1,0:T(8,128)S(1)} collective-permute-done((f32[3,160,128]{2,1,0:T(8,128)S(1)}, f32[3,160,128]{2,1,0:T(8,128)S(1)}, u32[]{:S(2)}, u32[]{:S(2)}) %collective-permute-start.3) | collective-permute-done | bytes 245792 | tf_op jit(solution)/shard_map/ppermute | solution.py:19
  200.6 1.0 fusion.44
  201.6 0.0 copy-done.2
  201.6 0.7 fusion.45
  (1 shorter events, 0.0 us)
Async XLA Ops:
  8.0 17.1 %copy-start.1 = (f32[2,256,256]{2,1,0:T(8,128)S(1)}, f32[2,256,256]{2,1,0:T(8,128)}, u32[]{:S(2)}) copy-start(f32[2,256,256]{2,1,0:T(8,128)} %param.15) | copy-start | bytes 1572868
  8.0 175.3 %all-reduce.3.cloned.1.call-start = ((), (), s32[]{:S(2)}) async-start(), calls=%async_computation.2 | async-start | bytes 1572864 | tf_op jit(solution)/shard_map/psum | solution.py:132
  14.1 9.4 %collective-permute-start.1 = (f32[2,320,128]{2,1,0:T(8,128)S(1)}, f32[2,320,128]{2,1,0:T(8,128)S(1)}, u32[]{:S(2)}, u32[]{:S(2)}) collective-permute-start(f32[2,320,128]{2,1,0:T(8,128)S(1)} %all_gather.3), channel_id=1, source_target_pairs={{2,0},{4,2},{6,4},{8,6},{10,8},{12,10},{14,12},{16,14},{18,16},{20... | collective-permute-start | bytes 983048 | tf_op jit(solution)/shard_map/ppermute | solution.py:19
  17.6 7.1 %collective-permute-start = (f32[2,320,128]{2,1,0:T(8,128)S(1)}, f32[2,320,128]{2,1,0:T(8,128)S(1)}, u32[]{:S(2)}, u32[]{:S(2)}) collective-permute-start(f32[2,320,128]{2,1,0:T(8,128)S(1)} %all_gather.3), channel_id=1, source_target_pairs={{0,2},{2,4},{4,6},{6,8},{8,10},{10,12},{12,14},{14,16},{16,18},{18... | collective-permute-start | bytes 983048 | tf_op jit(solution)/shard_map/ppermute | solution.py:18
  32.6 3.0 %copy-start.4 = (f32[1,256,256]{2,1,0:T(8,128)S(1)}, f32[1,256,256]{2,1,0:T(8,128)}, u32[]{:S(2)}) copy-start(f32[1,256,256]{2,1,0:T(8,128)} %param.16) | copy-start | bytes 786436
  51.1 135.5 %reduce-scatter.2.cloned.1.call-start = ((), (), s32[]{:S(2)}) async-start(), calls=%async_computation.1 | async-start | bytes 2211840 | tf_op jit(solution)/shard_map/reduce_scatter | solution.py:129
  61.9 1.1 copy-start
  183.3 10.9 %copy-start.3 = (f32[2,256,256]{2,1,0:T(8,128)S(1)}, f32[2,256,256]{2,1,0:T(8,128)}, u32[]{:S(2)}) copy-start(f32[2,256,256]{2,1,0:T(8,128)} %get-tuple-element.71) | copy-start | bytes 1572868
  187.7 7.6 %collective-permute-start.2 = (f32[3,160,128]{2,1,0:T(8,128)S(1)}, f32[3,160,128]{2,1,0:T(8,128)S(1)}, u32[]{:S(2)}, u32[]{:S(2)}) collective-permute-start(f32[3,160,128]{2,1,0:T(8,128)S(1)} %get-tuple-element.81), channel_id=1, source_target_pairs={{0,2},{2,4},{4,6},{6,8},{8,10},{10,12},{12,14},{14,16},{16,18},{18... | collective-permute-start | bytes 737288 | tf_op jit(solution)/shard_map/ppermute | solution.py:18
  192.2 8.4 %collective-permute-start.3 = (f32[3,160,128]{2,1,0:T(8,128)S(1)}, f32[3,160,128]{2,1,0:T(8,128)S(1)}, u32[]{:S(2)}, u32[]{:S(2)}) collective-permute-start(f32[3,160,128]{2,1,0:T(8,128)S(1)} %get-tuple-element.82), channel_id=1, source_target_pairs={{2,0},{4,2},{6,4},{8,6},{10,8},{12,10},{14,12},{16,14},{18,16},{20... | collective-permute-start | bytes 737288 | tf_op jit(solution)/shard_map/ppermute | solution.py:19
  194.1 7.5 %copy-start.2 = (f32[2,160,128]{2,1,0:T(8,128)S(1)}, f32[2,160,128]{2,1,0:T(8,128)}, u32[]{:S(2)}) copy-start(f32[2,160,128]{2,1,0:T(8,128)} %param.14) | copy-start | bytes 491524
Sparse Core Ops, SparseCore 0:
  51.2 131.9 all-reduce.2
Sparse Core Ops, SparseCore 1:
  63.1 27.8 reduce-scatter.1
where the time goes:
time: 210 us
  waiting for transfers between devices  127 us (60%)
  matrix products  24.1 us (11%)
  between operations  19 us (9%)
  starting transfers between devices  13 us (6%)
  local copies, waits for them, and re-layouts  12.2 us (6%)
  other arithmetic  8.07 us (4%)
  blocking collectives  6.09 us (3%)
    psum x1, waiting for transfers between devices, local(): lax.psum((probe_grad, window_light), ('tile', 'group'))  120 us
    dot_general x8, matrix products, apply_right(): jnp.einsum('pjk,kl->pjl', values, matrix, precision=lax.Precision.HIGHEST)  12.3 us
    dot_general x8, matrix products, apply_left(): jnp.einsum('jk,pkl->pjl', matrix, values, precision=lax.Precision.HIGHEST)  11.8 us
    dynamic_update_slice x1, local copies, waits for them, and re-layouts, place(): return lax.dynamic_update_slice(current, piece + terms[slot], corner)  9.85 us
    ppermute x2, starting transfers between devices, padded_2(): before = lax.ppermute(last, axis, up)  7.55 us
    ppermute x2, waiting for transfers between devices, padded_2(): after = lax.ppermute(initial, axis, down)  6.25 us
    all_gather x1, blocking collectives, local(): full_rows = lax.all_gather(object_field, 'group', axis=1, tiled=True)  6.09 us
    ppermute x2, starting transfers between devices, padded_2(): after = lax.ppermute(initial, axis, down)  5.35 us
  transfers between devices with their start and end apart: 6, of which 5 were waited for; matrix products, arithmetic and copies ran while one was open for 7% of the time, Pallas kernels for 0%

commit v1 on v0

--- a/solution.py
+++ b/solution.py
@@ -129,7 +129,7 @@
     reduced = lax.psum_scatter(accum, "group", scatter_dimension=1, tiled=True)
     arrived = padded_2(edge_strips(reduced), (("tile", 2),), HALO)
     share = add_edges(reduced[:, :, HALO : reduced.shape[2] - HALO], arrived)
-    probe_grad, window_light = lax.psum((probe_grad, window_light), ("tile", "group"))
+    probe_grad, window_light = lax.psum(lax.psum((probe_grad, window_light), "group"), "tile")
     object_field, probe_field = apply_updates(
         object_field, probe_field, share, probe_grad, window_light
     )

time: 210 us -> 232 us (1.10)
  waiting for transfers between devices: 127 us -> 151 us
    reduce_scatter x1, waiting for transfers between devices: 0.03 us -> 24.7 us  [local(): reduced = lax.psum_scatter(accum, 'group', scatter_dimension=1, tiled=True)]
    psum x1 -> x2, waiting for transfers between devices: 120 us -> 119 us  [the longest x1 82.2 us: local(): lax.psum(lax.psum((probe_grad, window_light), 'group'), 'tile')]
  transfers between devices with their start and end apart: 6 -> 7, of which waited for: 5 -> 7; matrix products, arithmetic and copies ran while one was open for 7% -> 6% of each run, Pallas kernels for 0% -> 0%
where the time goes in v1:
time: 232 us
  waiting for transfers between devices  151 us (65%)
  matrix products  24.1 us (10%)
  between operations  17.3 us (7%)
  starting transfers between devices  12.4 us (5%)
  local copies, waits for them, and re-layouts  12.2 us (5%)
  other arithmetic  8.11 us (3%)
  blocking collectives  6.09 us (3%)
    psum x1, waiting for transfers between devices, local(): lax.psum(lax.psum((probe_grad, window_light), 'group'), 'tile')  82.2 us
    psum x1, waiting for transfers between devices, local(): lax.psum((probe_grad, window_light), 'group')  36.8 us
    reduce_scatter x1, waiting for transfers between devices, local(): reduced = lax.psum_scatter(accum, 'group', scatter_dimension=1, tiled=True)  24.7 us
    dot_general x8, matrix products, apply_right(): jnp.einsum('pjk,kl->pjl', values, matrix, precision=lax.Precision.HIGHEST)  12.3 us
    dot_general x8, matrix products, apply_left(): jnp.einsum('jk,pkl->pjl', matrix, values, precision=lax.Precision.HIGHEST)  11.8 us
    dynamic_update_slice x1, local copies, waits for them, and re-layouts, place(): return lax.dynamic_update_slice(current, piece + terms[slot], corner)  9.85 us
    ppermute x2, starting transfers between devices, padded_2(): before = lax.ppermute(last, axis, up)  6.92 us
    ppermute x2, waiting for transfers between devices, padded_2(): after = lax.ppermute(initial, axis, down)  6.26 us
  transfers between devices with their start and end apart: 7, of which 7 were waited for; matrix products, arithmetic and copies ran while one was open for 6% of the time, Pallas kernels for 0%

profile of v1, /device:TPU:3, one launch (start us, length us, event | category | flops | bytes accessed | tf_op | source)
XLA Modules:
  0.0 231.6 jit_solution(10477526555658630507)
XLA Ops:
  7.2 0.0 copy-start.1
  7.2 0.0 all-reduce.7.cloned.1.call-start
  7.2 6.1 %all_gather.3 = f32[2,320,128]{2,1,0:T(8,128)S(1)} all-gather(f32[2,160,128]{2,1,0:T(8,128)} %param.14), channel_id=1, replica_groups=mesh['tile'=16,'group'=2] {'group'}, dimensions={1}, use_global_device_ids=true | all-gather | bytes 491520 | tf_op jit(solution)/shard_map/all_gather | solution.py:121
  13.3 3.4 %collective-permute-start.1 = (f32[2,320,128]{2,1,0:T(8,128)S(1)}, f32[2,320,128]{2,1,0:T(8,128)S(1)}, u32[]{:S(2)}, u32[]{:S(2)}) collective-permute-start(f32[2,320,128]{2,1,0:T(8,128)S(1)} %all_gather.3), channel_id=1, source_target_pairs={{2,0},{4,2},{6,4},{8,6},{10,8},{12,10},{14,12},{16,14},{18,16},{20... | collective-permute-start | bytes 983048 | tf_op jit(solution)/shard_map/ppermute | solution.py:19
  16.7 3.1 %collective-permute-start = (f32[2,320,128]{2,1,0:T(8,128)S(1)}, f32[2,320,128]{2,1,0:T(8,128)S(1)}, u32[]{:S(2)}, u32[]{:S(2)}) collective-permute-start(f32[2,320,128]{2,1,0:T(8,128)S(1)} %all_gather.3), channel_id=1, source_target_pairs={{0,2},{2,4},{4,6},{6,8},{8,10},{10,12},{12,14},{14,16},{16,18},{18... | collective-permute-start | bytes 983048 | tf_op jit(solution)/shard_map/ppermute | solution.py:18
  21.8 1.0 collective-permute-done.1
  22.7 1.1 collective-permute-done
  23.9 0.4 fusion.12
  24.3 0.0 copy-done.1
  24.3 0.1 fusion.39
  24.4 1.5 fusion.37
  25.9 1.5 fusion.33
  27.3 1.5 fusion.9
  28.8 1.5 fusion.7
  30.3 1.5 fusion.48
  31.8 0.0 copy-start.4
  31.8 1.5 fusion.49
  33.3 1.5 fusion.4
  34.8 0.0 copy-done.4
  34.8 1.7 bitcast_multiply_fusion.11
  36.5 1.5 fusion.30
  38.0 1.5 fusion.26
  39.5 1.5 fusion.3
  41.0 1.5 fusion.2
  42.5 1.5 fusion.46
  44.0 1.5 fusion.47
  45.4 1.5 fusion
  46.9 1.7 fusion.1
  48.6 0.8 fusion.17
  49.5 0.8 pad_maximum_fusion
  50.3 0.0 all-reduce.7.cloned.1.call-update
  50.3 0.0 all-reduce.5.cloned.1.call-start
  50.4 36.8 %all-reduce.7.cloned.1.call-done = (f32[2,256,256]{2,1,0:T(8,128)}, f32[256,256]{1,0:T(8,128)}) async-done(((f32[2,256,256]{2,1,0:T(8,128)}, f32[256,256]{1,0:T(8,128)}), (f32[2,256,256]{2,1,0:T(8,128)}, f32[256,256]{1,0:T(8,128)})) %all-reduce.7.cloned.1.call-update) | async-done | bytes 786448 | tf_op jit(solution)/shard_map/psum | solution.py:132
  87.2 0.0 all-reduce.5.cloned.1.call-update
  87.2 0.0 reduce-scatter.2.cloned.1.call-start
  87.3 0.7 fusion.23
  88.0 0.1 maximum_bitcast_fusion
  88.0 0.1 broadcast_in_dim.6
  88.1 9.9 %dynamic_update_slice.4 = f32[3,320,384]{2,1,0:T(8,128)S(1)} dynamic-update-slice(f32[3,320,384]{2,1,0:T(8,128)S(1)} %broadcast_in_dim.6, f32[3,256,256]{2,1,0:T(8,128)S(1)} %maximum_bitcast_fusion, s32[]{:T(128)} %constant.112.clone.1, s32[]{:T(128)S(6)} %select_n.60, s32[]{:T(128)S(6)} %select_n.61) | dynamic-update-slice | bytes 1572868 | tf_op jit(solution)/shard_map/while/body/eval_jaxpr/dynamic_update_slice | solution.py:86
  98.0 0.0 copy-start
  98.0 1.1 copy-done
  99.1 0.0 reduce-scatter.2.cloned.1.call-update
  99.8 82.2 %all-reduce.5.cloned.1.call-done = (f32[2,256,256]{2,1,0:T(8,128)}, f32[256,256]{1,0:T(8,128)}) async-done(((f32[2,256,256]{2,1,0:T(8,128)}, f32[256,256]{1,0:T(8,128)}), (f32[2,256,256]{2,1,0:T(8,128)}, f32[256,256]{1,0:T(8,128)})) %all-reduce.5.cloned.1.call-update) | async-done | bytes 786448 | tf_op jit(solution)/shard_map/psum | solution.py:132
  182.0 0.0 copy-start.3
  182.0 1.7 reduce_sum.8
  184.4 1.0 add_add_fusion
  185.4 24.7 %reduce-scatter.2.cloned.1.call-done = f32[3,160,384]{2,1,0:T(8,128)} async-done(((f32[3,320,384]{2,1,0:T(8,128)}), f32[3,160,384]{2,1,0:T(8,128)}) %reduce-scatter.2.cloned.1.call-update) | async-done | bytes 737296 | tf_op jit(solution)/shard_map/reduce_scatter | solution.py:129
  210.0 1.1 fusion.132
  211.1 3.8 %collective-permute-start.2 = (f32[3,160,128]{2,1,0:T(8,128)S(1)}, f32[3,160,128]{2,1,0:T(8,128)S(1)}, u32[]{:S(2)}, u32[]{:S(2)}) collective-permute-start(f32[3,160,128]{2,1,0:T(8,128)S(1)} %get-tuple-element.83), channel_id=1, source_target_pairs={{0,2},{2,4},{4,6},{6,8},{8,10},{10,12},{12,14},{14,16},{16,18},{18... | collective-permute-start | bytes 737288 | tf_op jit(solution)/shard_map/ppermute | solution.py:18
  215.0 1.9 collective-permute-start.3
  216.9 0.0 copy-done.3
  216.9 0.0 copy-start.2
  216.9 0.9 divide_subtract_fusion
  217.8 0.3 collective-permute-done.2
  218.1 5.3 %collective-permute-done.3 = f32[3,160,128]{2,1,0:T(8,128)S(1)} collective-permute-done((f32[3,160,128]{2,1,0:T(8,128)S(1)}, f32[3,160,128]{2,1,0:T(8,128)S(1)}, u32[]{:S(2)}, u32[]{:S(2)}) %collective-permute-start.3) | collective-permute-done | bytes 245792 | tf_op jit(solution)/shard_map/ppermute | solution.py:19
  223.4 1.0 fusion.44
  224.4 0.0 copy-done.2
  224.4 0.7 fusion.45
  (1 shorter events, 0.0 us)
Async XLA Ops:
  7.2 17.1 %copy-start.1 = (f32[2,256,256]{2,1,0:T(8,128)S(1)}, f32[2,256,256]{2,1,0:T(8,128)}, u32[]{:S(2)}) copy-start(f32[2,256,256]{2,1,0:T(8,128)} %param.15) | copy-start | bytes 1572868
  7.2 80.0 %all-reduce.7.cloned.1.call-start = ((), (), s32[]{:S(2)}) async-start(), calls=%async_computation.3 | async-start | bytes 1572864 | tf_op jit(solution)/shard_map/psum | solution.py:132
  13.3 9.4 %collective-permute-start.1 = (f32[2,320,128]{2,1,0:T(8,128)S(1)}, f32[2,320,128]{2,1,0:T(8,128)S(1)}, u32[]{:S(2)}, u32[]{:S(2)}) collective-permute-start(f32[2,320,128]{2,1,0:T(8,128)S(1)} %all_gather.3), channel_id=1, source_target_pairs={{2,0},{4,2},{6,4},{8,6},{10,8},{12,10},{14,12},{16,14},{18,16},{20... | collective-permute-start | bytes 983048 | tf_op jit(solution)/shard_map/ppermute | solution.py:19
  16.7 7.1 %collective-permute-start = (f32[2,320,128]{2,1,0:T(8,128)S(1)}, f32[2,320,128]{2,1,0:T(8,128)S(1)}, u32[]{:S(2)}, u32[]{:S(2)}) collective-permute-start(f32[2,320,128]{2,1,0:T(8,128)S(1)} %all_gather.3), channel_id=1, source_target_pairs={{0,2},{2,4},{4,6},{6,8},{8,10},{10,12},{12,14},{14,16},{16,18},{18... | collective-permute-start | bytes 983048 | tf_op jit(solution)/shard_map/ppermute | solution.py:18
  31.8 3.0 %copy-start.4 = (f32[1,256,256]{2,1,0:T(8,128)S(1)}, f32[1,256,256]{2,1,0:T(8,128)}, u32[]{:S(2)}) copy-start(f32[1,256,256]{2,1,0:T(8,128)} %param.16) | copy-start | bytes 786436
  50.3 131.7 %all-reduce.5.cloned.1.call-start = ((), (), s32[]{:S(2)}) async-start(), calls=%async_computation.2 | async-start | bytes 1572864 | tf_op jit(solution)/shard_map/psum | solution.py:132
  87.2 122.8 %reduce-scatter.2.cloned.1.call-start = ((), (), s32[]{:S(2)}) async-start(), calls=%async_computation.1 | async-start | bytes 2211840 | tf_op jit(solution)/shard_map/reduce_scatter | solution.py:129
  98.0 1.1 copy-start
  182.0 34.9 %copy-start.3 = (f32[2,256,256]{2,1,0:T(8,128)S(1)}, f32[2,256,256]{2,1,0:T(8,128)}, u32[]{:S(2)}) copy-start(f32[2,256,256]{2,1,0:T(8,128)} %get-tuple-element.71) | copy-start | bytes 1572868
  211.1 7.0 %collective-permute-start.2 = (f32[3,160,128]{2,1,0:T(8,128)S(1)}, f32[3,160,128]{2,1,0:T(8,128)S(1)}, u32[]{:S(2)}, u32[]{:S(2)}) collective-permute-start(f32[3,160,128]{2,1,0:T(8,128)S(1)} %get-tuple-element.83), channel_id=1, source_target_pairs={{0,2},{2,4},{4,6},{6,8},{8,10},{10,12},{12,14},{14,16},{16,18},{18... | collective-permute-start | bytes 737288 | tf_op jit(solution)/shard_map/ppermute | solution.py:18
  215.0 8.4 %collective-permute-start.3 = (f32[3,160,128]{2,1,0:T(8,128)S(1)}, f32[3,160,128]{2,1,0:T(8,128)S(1)}, u32[]{:S(2)}, u32[]{:S(2)}) collective-permute-start(f32[3,160,128]{2,1,0:T(8,128)S(1)} %get-tuple-element.84), channel_id=1, source_target_pairs={{2,0},{4,2},{6,4},{8,6},{10,8},{12,10},{14,12},{16,14},{18,16},{20... | collective-permute-start | bytes 737288 | tf_op jit(solution)/shard_map/ppermute | solution.py:19
  216.9 7.5 %copy-start.2 = (f32[2,160,128]{2,1,0:T(8,128)S(1)}, f32[2,160,128]{2,1,0:T(8,128)}, u32[]{:S(2)}) copy-start(f32[2,160,128]{2,1,0:T(8,128)} %param.14) | copy-start | bytes 491524
Sparse Core Ops, SparseCore 0:
  50.4 36.7 all-reduce.6
  90.7 91.2 all-reduce.4
  184.3 25.6 reduce-scatter.1
